TPU v7x, 32 devices: a whole 2x2x4 slice. The times are simulated.
32 devices in a mesh: seq: 4 (over z), shard: 8 (over y, x, core).
Axes of the slice: x: 2, y: 2, z: 4, core: 2. Of those that a mesh axis runs over, the one named last changes fastest.
Arguments:
- frames: bfloat16 [8, 1024, 1536], P('shard', 'seq'), may hold values from -6 to 6
- text_states: bfloat16 [8, 64, 1536], P('shard'), may hold values from -6 to 6
- norm_gain: bfloat16 [3, 1536], P(None, 'shard'), may hold values from 0.5 to 1.5
- norm_bias: bfloat16 [3, 1536], P(None, 'shard'), may hold values from -3 to 3
- self_project: bfloat16 [3, 1536, 1536], P(None, 'shard'), may hold values from -0.15625 to 0.15625
- self_output: bfloat16 [1536, 1536], P('shard'), may hold values from -1.75 to 1.75
- cross_project: bfloat16 [3, 1536, 1536], P(None, 'shard'), may hold values from -0.15625 to 0.15625
- cross_output: bfloat16 [1536, 1536], P('shard'), may hold values from -0.625 to 0.625
- up_weight: bfloat16 [1536, 6144], P('shard'), may hold values from -0.15625 to 0.15625
- down_weight: bfloat16 [6144, 1536], P('shard'), may hold values from -0.078125 to 0.078125
- cotangent: bfloat16 [8, 1024, 1536], P('shard', 'seq'), may hold values from -6 to 6
Outputs:
- output: bfloat16 [8, 1024, 1536], P('shard', 'seq')
- frames_grad: float32 [8, 1024, 1536], P('shard', 'seq')
- text_grad: float32 [8, 64, 1536], P('shard')
- gain_grad: float32 [3, 1536], P(None, 'shard')
- bias_grad: float32 [3, 1536], P(None, 'shard')
- self_project_grad: float32 [3, 1536, 1536], P(None, 'shard')
- self_output_grad: float32 [1536, 1536], P('shard')
- cross_project_grad: float32 [3, 1536, 1536], P(None, 'shard')
- cross_output_grad: float32 [1536, 1536], P('shard')
- up_grad: float32 [1536, 6144], P('shard')
- down_grad: float32 [6144, 1536], P('shard')
All inputs are finite; a program needn't handle non-finite values.
Results may differ from a plain program's by a relative error of at most 0.022.
Values may be sent and summed in bfloat16 or wider, within the bound.
No kernel may reach another device: no remote copies, remote signals or barrier semaphores. Data moves between devices by JAX's collectives and lax.ppermute only.
A program may use at most 384 MiB of HBM per device.

v0:
```python
import jax
import jax.numpy as jnp
from jax import lax
from jax.sharding import PartitionSpec as P

HEAD_DIM = 64
QBLOCK = 512
EPSILON = 1e-05
MASKED_SCORE = -1e30


def layer_norm(hidden, gain, shift):
    center = hidden - jnp.mean(hidden, axis=-1, keepdims=True)
    spread = lax.rsqrt(jnp.mean(center * center, axis=-1, keepdims=True) + EPSILON)
    return center * spread * gain + shift


def exact_gelu(values):
    return jax.nn.gelu(values, approximate=False)


def contract(form, left, right):
    return jnp.einsum(form, left, right, preferred_element_type=jnp.float32)


def split_heads(values):
    return values.reshape(values.shape[:-1] + (values.shape[-1] // HEAD_DIM, HEAD_DIM))


def join_heads(values):
    return values.reshape(values.shape[:-2] + (values.shape[-2] * values.shape[-1],))


def causal_visible(start_row, row_count, stop_row):
    row_place = start_row + lax.broadcasted_iota(jnp.int32, (row_count, stop_row), 0)
    column_place = lax.broadcasted_iota(jnp.int32, (row_count, stop_row), 1)
    return column_place <= row_place


def block_scores(queries, key_rows, start_row, stop_row, scaling):
    scores = (
        contract("cqhe,ckhe->chqk", queries[:, start_row:stop_row], key_rows[:, :stop_row])
        * scaling
    )
    return jnp.where(
        causal_visible(start_row, stop_row - start_row, stop_row), scores, MASKED_SCORE
    )


def self_forward(queries, key_rows, value_rows, scaling):
    length = queries.shape[1]
    outputs = []
    totals = []
    for start_row in range(0, length, QBLOCK):
        stop_row = start_row + QBLOCK
        scores = block_scores(queries, key_rows, start_row, stop_row, scaling)
        largest = jnp.max(scores, axis=-1, keepdims=True)
        weights = jnp.exp(scores - largest)
        summed = jnp.sum(weights, axis=-1, keepdims=True)
        shares = (weights / summed).astype(jnp.bfloat16)
        outputs.append(contract("chqk,ckhe->cqhe", shares, value_rows[:, :stop_row]))
        totals.append(largest + jnp.log(summed))
    return (jnp.concatenate(outputs, axis=1), totals)


def self_backward(queries, key_rows, value_rows, totals, grad_out, scaling):
    length = queries.shape[1]
    grad_queries = []
    grad_keys = jnp.zeros(key_rows.shape, jnp.float32)
    grad_values = jnp.zeros(value_rows.shape, jnp.float32)
    for number, start_row in enumerate(range(0, length, QBLOCK)):
        stop_row = start_row + QBLOCK
        query_block = queries[:, start_row:stop_row]
        grad_block = grad_out[:, start_row:stop_row]
        scores = block_scores(queries, key_rows, start_row, stop_row, scaling)
        shares = jnp.exp(scores - totals[number])
        grad_shares = contract("cqhe,ckhe->chqk", grad_block, value_rows[:, :stop_row])
        centred = jnp.sum(shares * grad_shares, axis=-1, keepdims=True)
        grad_scores = (shares * (grad_shares - centred)).astype(jnp.bfloat16)
        grad_queries.append(
            contract("chqk,ckhe->cqhe", grad_scores, key_rows[:, :stop_row]) * scaling
        )
        grad_keys = grad_keys.at[:, :stop_row].add(
            contract("chqk,cqhe->ckhe", grad_scores, query_block) * scaling
        )
        grad_values = grad_values.at[:, :stop_row].add(
            contract("chqk,cqhe->ckhe", shares.astype(jnp.bfloat16), grad_block)
        )
    return (jnp.concatenate(grad_queries, axis=1), grad_keys, grad_values)


def cross_softmax(queries, key_rows, scaling):
    scores = contract("cfhe,cxhe->chxf", queries, key_rows) * scaling
    largest = jnp.max(scores, axis=2, keepdims=True)
    weights = jnp.exp(scores - largest)
    return weights / jnp.sum(weights, axis=2, keepdims=True)


def fetch_self(self_project, self_output, norm_gain, norm_bias):
    return (
        lax.all_gather(self_project, "shard", axis=1, tiled=True),
        lax.all_gather(self_output, "shard", axis=0, tiled=True),
        lax.all_gather(norm_gain, "shard", axis=1, tiled=True),
        lax.all_gather(norm_bias, "shard", axis=1, tiled=True),
    )


def fetch_cross(cross_project, cross_output):
    return (
        lax.all_gather(cross_project, "shard", axis=1, tiled=True),
        lax.all_gather(cross_output, "shard", axis=0, tiled=True),
    )


def fetch_mlp(up_weight, down_weight):
    return (
        lax.all_gather(up_weight, "shard", axis=0, tiled=True),
        lax.all_gather(down_weight, "shard", axis=0, tiled=True),
    )


def body(
    frames,
    text_states,
    norm_gain,
    norm_bias,
    self_project,
    self_output,
    cross_project,
    cross_output,
    up_weight,
    down_weight,
    cotangent,
):
    scaling = HEAD_DIM ** (-0.5)
    project_all, output_all, gain_all, bias_all = fetch_self(
        self_project, self_output, norm_gain, norm_bias
    )
    gains = gain_all.astype(jnp.float32)
    biases = bias_all.astype(jnp.float32)
    hidden = frames.astype(jnp.float32)
    normed_one, norm_pull_one = jax.vjp(layer_norm, hidden, gains[0], biases[0])
    inputs_one = normed_one.astype(jnp.bfloat16)
    projected = contract("cfd,jde->jcfe", inputs_one, project_all).astype(jnp.bfloat16)
    by_heads = lax.all_to_all(projected, "seq", split_axis=3, concat_axis=2, tiled=True)
    queries = split_heads(by_heads[0])
    key_rows = split_heads(by_heads[1])
    value_rows = split_heads(by_heads[2])
    attended_heads, totals = self_forward(queries, key_rows, value_rows, scaling)
    attended = lax.all_to_all(
        join_heads(attended_heads).astype(jnp.bfloat16),
        "seq",
        split_axis=1,
        concat_axis=2,
        tiled=True,
    )
    hidden_one = hidden + contract("cfd,de->cfe", attended, output_all)
    cross_all, cross_out_all = fetch_cross(cross_project, cross_output)
    normed_two, norm_pull_two = jax.vjp(layer_norm, hidden_one, gains[1], biases[1])
    inputs_two = normed_two.astype(jnp.bfloat16)
    cross_queries = contract("cfd,de->cfe", inputs_two, cross_all[0]).astype(jnp.bfloat16)
    cross_pairs = contract("cxd,jde->jcxe", text_states, cross_all[1:]).astype(jnp.bfloat16)
    text_keys = split_heads(cross_pairs[0])
    text_values = split_heads(cross_pairs[1])
    cross_shares = cross_softmax(split_heads(cross_queries), text_keys, scaling)
    cross_low = cross_shares.astype(jnp.bfloat16)
    mixed_text = join_heads(contract("chxf,cxhe->cfhe", cross_low, text_values)).astype(
        jnp.bfloat16
    )
    hidden_two = hidden_one + contract("cfd,de->cfe", mixed_text, cross_out_all)
    up_all, down_all = fetch_mlp(up_weight, down_weight)
    normed_three, norm_pull_three = jax.vjp(layer_norm, hidden_two, gains[2], biases[2])
    inputs_three = normed_three.astype(jnp.bfloat16)
    before_act = contract("cfd,dk->cfk", inputs_three, up_all)
    activated, gelu_pull = jax.vjp(exact_gelu, before_act)
    activated_low = activated.astype(jnp.bfloat16)
    result = hidden_two + contract("cfk,kd->cfd", activated_low, down_all)
    output = result.astype(jnp.bfloat16)
    up_all, down_all = fetch_mlp(up_weight, down_weight)
    grad_result = cotangent.astype(jnp.float32)
    grad_down = contract("cfk,cfd->kd", activated_low, cotangent)
    grad_act = contract("cfd,kd->cfk", cotangent, down_all)
    grad_before = gelu_pull(grad_act)[0].astype(jnp.bfloat16)
    grad_up = contract("cfd,cfk->dk", inputs_three, grad_before)
    grad_inputs_three = contract("cfk,dk->cfd", grad_before, up_all)
    grad_two_part, gain_three, bias_three = norm_pull_three(grad_inputs_three)
    grad_hidden_two = grad_result + grad_two_part
    up_share, down_share = (
        lax.psum_scatter(
            grad_up.astype(jnp.bfloat16), "shard", scatter_dimension=0, tiled=True
        ).astype(jnp.float32),
        lax.psum_scatter(
            grad_down.astype(jnp.bfloat16), "shard", scatter_dimension=0, tiled=True
        ).astype(jnp.float32),
    )
    cross_all, cross_out_all = fetch_cross(cross_project, cross_output)
    grad_low_two = grad_hidden_two.astype(jnp.bfloat16)
    grad_cross_out = contract("cfd,cfe->de", mixed_text, grad_low_two)
    grad_mixed = split_heads(
        contract("cfe,de->cfd", grad_low_two, cross_out_all).astype(jnp.bfloat16)
    )
    grad_shares = contract("cfhe,cxhe->chxf", grad_mixed, text_values)
    centred = jnp.sum(cross_shares * grad_shares, axis=2, keepdims=True)
    grad_scores = (cross_shares * (grad_shares - centred)).astype(jnp.bfloat16)
    grad_cross_query = join_heads(
        contract("chxf,cxhe->cfhe", grad_scores, text_keys) * scaling
    ).astype(jnp.bfloat16)
    grad_text_keys = join_heads(
        contract("chxf,cfhe->cxhe", grad_scores, split_heads(cross_queries)) * scaling
    )
    grad_text_values = join_heads(contract("chxf,cfhe->cxhe", cross_low, grad_mixed))
    grad_pairs = lax.psum(jnp.stack([grad_text_keys, grad_text_values]).astype(jnp.bfloat16), "seq")
    grad_text = contract("jcxe,jde->cxd", grad_pairs, cross_all[1:])
    grad_cross_pairs = contract("cxd,jcxe->jde", text_states, grad_pairs)
    grad_cross_first = contract("cfd,cfe->de", inputs_two, grad_cross_query)
    grad_inputs_two = contract("cfe,de->cfd", grad_cross_query, cross_all[0])
    grad_one_part, gain_two, bias_two = norm_pull_two(grad_inputs_two)
    grad_hidden_one = grad_hidden_two + grad_one_part
    cross_stack = jnp.concatenate([grad_cross_first[None], grad_cross_pairs], axis=0)
    cross_share, cross_out_share = (
        lax.psum_scatter(
            cross_stack.astype(jnp.bfloat16), "shard", scatter_dimension=1, tiled=True
        ).astype(jnp.float32),
        lax.psum_scatter(
            grad_cross_out.astype(jnp.bfloat16), "shard", scatter_dimension=0, tiled=True
        ).astype(jnp.float32),
    )
    project_all, output_all, gain_all, bias_all = fetch_self(
        self_project, self_output, norm_gain, norm_bias
    )
    grad_low_one = grad_hidden_one.astype(jnp.bfloat16)
    grad_self_out = contract("cfd,cfe->de", attended, grad_low_one)
    grad_attended = contract("cfe,de->cfd", grad_low_one, output_all).astype(jnp.bfloat16)
    grad_heads = lax.all_to_all(grad_attended, "seq", split_axis=2, concat_axis=1, tiled=True)
    grad_queries, grad_keys, grad_values = self_backward(
        queries, key_rows, value_rows, totals, split_heads(grad_heads), scaling
    )
    grad_stacked = jnp.stack(
        [join_heads(grad_queries), join_heads(grad_keys), join_heads(grad_values)]
    ).astype(jnp.bfloat16)
    grad_projected = lax.all_to_all(grad_stacked, "seq", split_axis=2, concat_axis=3, tiled=True)
    grad_self_project = contract("cfd,jcfe->jde", inputs_one, grad_projected)
    grad_inputs_one = contract("jcfe,jde->cfd", grad_projected, project_all)
    grad_zero_part, gain_one, bias_one = norm_pull_one(grad_inputs_one)
    grad_frames = grad_hidden_one + grad_zero_part
    gain_stack = jnp.stack([gain_one, gain_two, gain_three])
    bias_stack = jnp.stack([bias_one, bias_two, bias_three])
    project_share, output_share, gain_share, bias_share = (
        lax.psum_scatter(
            grad_self_project.astype(jnp.bfloat16), "shard", scatter_dimension=1, tiled=True
        ).astype(jnp.float32),
        lax.psum_scatter(
            grad_self_out.astype(jnp.bfloat16), "shard", scatter_dimension=0, tiled=True
        ).astype(jnp.float32),
        lax.psum_scatter(
            gain_stack.astype(jnp.bfloat16), "shard", scatter_dimension=1, tiled=True
        ).astype(jnp.float32),
        lax.psum_scatter(
            bias_stack.astype(jnp.bfloat16), "shard", scatter_dimension=1, tiled=True
        ).astype(jnp.float32),
    )
    summed_parts = (
        lax.psum(project_share.astype(jnp.bfloat16), "seq").astype(jnp.float32),
        lax.psum(output_share.astype(jnp.bfloat16), "seq").astype(jnp.float32),
        lax.psum(cross_share[:1].astype(jnp.bfloat16), "seq").astype(jnp.float32),
        lax.psum(cross_out_share.astype(jnp.bfloat16), "seq").astype(jnp.float32),
        lax.psum(up_share.astype(jnp.bfloat16), "seq").astype(jnp.float32),
        lax.psum(down_share.astype(jnp.bfloat16), "seq").astype(jnp.float32),
        lax.psum(gain_share.astype(jnp.bfloat16), "seq").astype(jnp.float32),
        lax.psum(bias_share.astype(jnp.bfloat16), "seq").astype(jnp.float32),
    )
    cross_final = jnp.concatenate([summed_parts[2], cross_share[1:]], axis=0)
    return (
        output,
        grad_frames,
        grad_text,
        summed_parts[6],
        summed_parts[7],
        summed_parts[0],
        summed_parts[1],
        cross_final,
        summed_parts[3],
        summed_parts[4],
        summed_parts[5],
    )


def solution(mesh):
    return jax.shard_map(
        body,
        mesh=mesh,
        in_specs=(
            P("shard", "seq", None),
            P("shard", None, None),
            P(None, "shard"),
            P(None, "shard"),
            P(None, "shard", None),
            P("shard", None),
            P(None, "shard", None),
            P("shard", None),
            P("shard", None),
            P("shard", None),
            P("shard", "seq", None),
        ),
        out_specs=(
            P("shard", "seq", None),
            P("shard", "seq", None),
            P("shard", None, None),
            P(None, "shard"),
            P(None, "shard"),
            P(None, "shard", None),
            P("shard", None),
            P(None, "shard", None),
            P("shard", None),
            P("shard", None),
            P("shard", None),
        ),
        check_vma=False,
    )
```

profile of v0, /device:TPU:0, one launch (start us, length us, event | category | flops | bytes accessed | tf_op | source)
XLA Modules:
  0.0 1739.3 jit_solution(10451731953631284153)
XLA Ops:
  11.2 10.4 all-gather
  21.7 9.2 all-gather.1
  31.7 59.6 %all-gather.9.cloned.1.call-done = bf16[3,1536,1536]{2,1,0:T(8,128)(2,1)} async-done(((bf16[3,192,1536]{2,1,0:T(8,128)(2,1)}), bf16[3,1536,1536]{2,1,0:T(8,128)(2,1)}) %all-gather.9.cloned.1.call-update) | async-done | bytes 14155792 | tf_op jit(solution)/shard_map/all_gather | solution.py:101
  91.4 9.3 fusion.27
  104.3 5.0 all-to-all-start
  111.2 69.5 %all-to-all-done = bf16[3,1,256,1536]{2,0,1,3:T(4,128)(2,1)} async-done(((bf16[3,1,256,1536]{2,0,1,3:T(4,128)(2,1)}), bf16[3,1,256,1536]{2,0,1,3:T(4,128)(2,1)}, u32[]{:S(2)}, u32[]{:S(2)}) %all-to-all-start) | async-done | bytes 2359328 | tf_op jit(solution)/shard_map/all_to_all | solution.py:145
  180.7 4.3 copy.243
  210.0 5.5 reduce.59
  220.0 6.0 fusion.41
  228.0 11.9 all-to-all-done.1
  241.3 4.2 fusion.120
  245.8 4.8 fusion.32
  256.7 4.1 fusion.122
  261.1 92.5 %all-gather.17.cloned.1.call-done = bf16[1536,6144]{1,0:T(8,128)(2,1)} async-done(((bf16[192,6144]{1,0:T(8,128)(2,1)}), bf16[1536,6144]{1,0:T(8,128)(2,1)}) %all-gather.17.cloned.1.call-update) | async-done | bytes 18874384 | tf_op jit(solution)/shard_map/all_gather | solution.py:117
  353.6 23.7 %multiply_convert_fusion.2 = (bf16[256,6144]{1,0:T(8,128)(2,1)}, f32[256,6144]{1,0:T(8,128)}, f32[256,6144]{1,0:T(8,128)}) fusion(bf16[1536,6144]{1,0:T(8,128)(2,1)} %all-gather.17.cloned.1.call-done, f32[1,256,1536]{2,1,0:T(8,128)S(1)} %get-tuple-element.192, f32[1536]{0:T(1024)S(1)} %get-tuple-element.161, f32[1536]{0:T(1024)S(1)} %get-tuple-element.206, ...), kind=kOutput, calls=%fused_computation.31 | convolution fusion | flops 4936040448 | bytes 36190208 | tf_op jit(solution)/shard_map/cfd,dk->cfk/dot_general | solution.py:23
  377.3 76.7 %all-gather.19.cloned.1.call-done = bf16[6144,1536]{1,0:T(8,128)(2,1)} async-done(((bf16[768,1536]{1,0:T(8,128)(2,1)}), bf16[6144,1536]{1,0:T(8,128)(2,1)}) %all-gather.19.cloned.1.call-update) | async-done | bytes 18874384 | tf_op jit(solution)/shard_map/all_gather | solution.py:118
  453.9 14.8 add_convert_fusion
  468.7 10.7 fusion.57
  482.4 4.8 convolution_convert_fusion.8
  506.5 7.0 copy.211
  513.5 24.0 %all-reduce.7.cloned.1.call-done = bf16[2,64,1536]{2,1,0:T(8,128)(2,1)} async-done(((bf16[2,64,1536]{2,1,0:T(8,128)(2,1)}), bf16[2,64,1536]{2,1,0:T(8,128)(2,1)}) %all-reduce.7.cloned.1.call-update) | async-done | bytes 393232 | tf_op jit(solution)/shard_map/psum | solution.py:212
  537.5 4.0 fusion.3
  541.6 6.1 pad_maximum_fusion
  547.7 30.8 %copy.225 = bf16[3,1536,1536]{2,0,1:T(4,128)(2,1)} copy(bf16[3,1536,1536]{1,2,0:T(8,128)(2,1)} %pad_maximum_fusion) | data formatting | bytes 28311552
  578.5 17.0 copy.233
  596.7 4.3 fusion.58
  607.5 8.2 reduce.60
  620.5 18.2 %all-to-all-done.2 = bf16[4,2,49152]{2,1,0:T(2,128)(2,1)S(1)} async-done(((bf16[4,2,49152]{2,1,0:T(2,128)(2,1)}), bf16[4,2,49152]{2,1,0:T(2,128)(2,1)S(1)}, u32[]{:S(2)}, u32[]{:S(2)}) %all-to-all-start.2) | async-done | bytes 786464 | tf_op jit(solution)/shard_map/all_to_all | solution.py:234
  641.0 4.2 fusion.64
  645.1 6.2 fusion.55
  654.2 6.9 multiply_reduce_fusion.1
  661.2 6.7 multiply_convert_fusion.1
  669.3 6.8 multiply_reduce_fusion
  676.1 6.2 multiply_convert_fusion
  685.3 5.0 copy.204
  691.9 4.9 fusion.74
  697.9 5.1 copy.203
  703.0 6.8 pad_maximum_fusion.1
  709.7 72.8 %all_to_all.60 = bf16[3,1,1024,384]{3,0,1,2:T(4,128)(2,1)S(1)} all-to-all(bf16[3,1,1024,384]{3,0,1,2:T(4,128)(2,1)S(1)} %pad_maximum_fusion.1), channel_id=1, replica_groups=mesh['seq'=4,'shard'=8] {'seq'}, dimensions={2} | all-to-all | bytes 4718592 | tf_op jit(solution)/shard_map/all_to_all | solution.py:241
  786.1 4.1 reshape.928
  790.3 7.5 convert_bitcast_fusion
  797.7 30.8 %copy.223 = bf16[3,1536,1536]{2,0,1:T(4,128)(2,1)} copy(bf16[3,1536,1536]{1,2,0:T(8,128)(2,1)} %convert_bitcast_fusion) | data formatting | bytes 28311552
  828.6 17.0 copy.232
  846.1 5.4 convolution_convert_fusion.3
  851.6 6.0 convolution_convert_fusion.5
  858.2 12.6 convolution_convert_fusion.1
  870.9 11.4 convolution_convert_fusion
  885.5 7.4 fusion.54
  897.2 3.8 reshape.947
  906.5 40.3 %reduce-scatter.29.cloned.1.call-done = bf16[192,4608]{1,0:T(8,128)(2,1)} async-done(((bf16[1536,4608]{1,0:T(8,128)(2,1)}), bf16[192,4608]{1,0:T(8,128)(2,1)}) %reduce-scatter.29.cloned.1.call-update) | async-done | bytes 1769488
  946.8 5.2 reshape.945
  951.9 5.6 copy.224
  957.5 46.9 %reduce-scatter.19.cloned.1.call-done = bf16[192,1536]{1,0:T(8,128)(2,1)} async-done(((bf16[1536,1536]{1,0:T(8,128)(2,1)}), bf16[192,1536]{1,0:T(8,128)(2,1)}) %reduce-scatter.19.cloned.1.call-update) | async-done | bytes 589840 | tf_op jit(solution)/shard_map/reduce_scatter | solution.py:224
  1004.5 57.8 %reduce-scatter.17.cloned.1.call-done = bf16[192,1536]{1,0:T(8,128)(2,1)} async-done(((bf16[1536,1536]{1,0:T(8,128)(2,1)}), bf16[192,1536]{1,0:T(8,128)(2,1)}) %reduce-scatter.17.cloned.1.call-update) | async-done | bytes 589840 | tf_op jit(solution)/shard_map/reduce_scatter | solution.py:252
  1062.3 129.9 %reduce-scatter.21.cloned.1.call-done = bf16[192,6144]{1,0:T(8,128)(2,1)} async-done(((bf16[1536,6144]{1,0:T(8,128)(2,1)}), bf16[192,6144]{1,0:T(8,128)(2,1)}) %reduce-scatter.21.cloned.1.call-update) | async-done | bytes 2359312 | tf_op jit(solution)/shard_map/reduce_scatter | solution.py:189
  1192.2 130.1 %reduce-scatter.23.cloned.1.call-done = bf16[768,1536]{1,0:T(8,128)(2,1)} async-done(((bf16[6144,1536]{1,0:T(8,128)(2,1)}), bf16[768,1536]{1,0:T(8,128)(2,1)}) %reduce-scatter.23.cloned.1.call-update) | async-done | bytes 2359312 | tf_op jit(solution)/shard_map/reduce_scatter | solution.py:192
  1323.7 10.7 fusion.31
  1334.4 7.6 fusion.44
  1343.7 15.4 reduce-scatter.25.cloned.1.call-done
  1360.0 35.9 %reduce-scatter.27.cloned.1.call-done = bf16[192,3]{1,0:T(8,128)(2,1)} async-done(((bf16[1536,3]{1,0:T(8,128)(2,1)}), bf16[192,3]{1,0:T(8,128)(2,1)}) %reduce-scatter.27.cloned.1.call-update) | async-done | bytes 1168
  1396.8 11.9 all-reduce.2
  1414.7 297.1 %all-reduce.9.cloned.1.call-done = (bf16[3,192,1536]{1,2,0:T(8,128)(2,1)}, bf16[192,1536]{1,0:T(8,128)(2,1)}, bf16[1,192,1536]{1,2,0:T(8,128)(2,1)}, bf16[192,15...) async-done(((bf16[3,192,1536]{1,2,0:T(8,128)(2,1)}, bf16[192,1536]{1,0:T(8,128)(2,1)}, bf16[1,192,1536]{1,2,0:T(8,128)(2,1)}, ...) | async-done | bytes 8257552 | tf_op jit(solution)/shard_map/psum | solution.py:263
  1711.8 4.5 copy.212
  1721.3 5.7 copy.213
  (340 shorter events, 135.1 us)
Async XLA Ops:
  7.2 212.9 %copy-start = (bf16[1,64,1536]{2,1,0:T(8,128)(2,1)S(1)}, bf16[1,64,1536]{2,1,0:T(8,128)(2,1)}, u32[]{:S(2)}) copy-start(bf16[1,64,1536]{2,1,0:T(8,128)(2,1)} %param.24) | copy-start | bytes 589828
  7.2 84.2 %all-gather.9.cloned.1.call-start = ((), (), s32[]{:S(2)}) async-start(), calls=%async_computation.12 | async-start | bytes 15925248 | tf_op jit(solution)/shard_map/all_gather | solution.py:101
  7.9 212.1 %all-gather.13.cloned.1.call-start = ((), (), s32[]{:S(2)}) async-start(), calls=%async_computation.14 | async-start | bytes 15925248 | tf_op jit(solution)/shard_map/all_gather | solution.py:110
  8.7 13.0 copy-start.90
  8.7 22.4 %copy-start.5 = (bf16[1,256,1536]{2,1,0:T(8,128)(2,1)S(1)}, bf16[1,256,1536]{2,1,0:T(8,128)(2,1)}, u32[]{:S(2)}) copy-start(bf16[1,256,1536]{2,1,0:T(8,128)(2,1)} %param.23) | copy-start | bytes 2359300
  8.7 232.6 %all-gather.11.cloned.1.call-start = ((), (), s32[]{:S(2)}) async-start(), calls=%async_computation.13 | async-start | bytes 5308416 | tf_op jit(solution)/shard_map/all_gather | solution.py:102
  9.4 247.2 %all-gather.15.cloned.1.call-start = ((), (), s32[]{:S(2)}) async-start(), calls=%async_computation.15 | async-start | bytes 5308416 | tf_op jit(solution)/shard_map/all_gather | solution.py:111
  10.0 343.6 %all-gather.17.cloned.1.call-start = ((), (), s32[]{:S(2)}) async-start(), calls=%async_computation.16 | async-start | bytes 21233664 | tf_op jit(solution)/shard_map/all_gather | solution.py:117
  10.6 443.3 %all-gather.19.cloned.1.call-start = ((), (), s32[]{:S(2)}) async-start(), calls=%async_computation.17 | async-start | bytes 21233664 | tf_op jit(solution)/shard_map/all_gather | solution.py:118
  31.1 69.6 %copy-start.54 = (f32[1536]{0:T(1024)}, f32[1536]{0:T(1024)S(1)}, u32[]{:S(2)}) copy-start(f32[1536]{0:T(1024)S(1)} %get-tuple-element.204) | copy-start | bytes 18436
  31.1 69.6 %copy-start.65 = (f32[1536]{0:T(1024)}, f32[1536]{0:T(1024)S(1)}, u32[]{:S(2)}) copy-start(f32[1536]{0:T(1024)S(1)} %get-tuple-element.163) | copy-start | bytes 18436
  31.1 214.7 %copy-start.67 = (f32[1536]{0:T(1024)}, f32[1536]{0:T(1024)S(1)}, u32[]{:S(2)}) copy-start(f32[1536]{0:T(1024)S(1)} %get-tuple-element.205) | copy-start | bytes 18436
  31.1 214.7 %copy-start.83 = (f32[1536]{0:T(1024)}, f32[1536]{0:T(1024)S(1)}, u32[]{:S(2)}) copy-start(f32[1536]{0:T(1024)S(1)} %get-tuple-element.162) | copy-start | bytes 18436
  31.1 322.4 %copy-start.56 = (f32[1536]{0:T(1024)}, f32[1536]{0:T(1024)S(1)}, u32[]{:S(2)}) copy-start(f32[1536]{0:T(1024)S(1)} %get-tuple-element.161) | copy-start | bytes 18436
  31.4 69.4 %copy-start.70 = (f32[256]{0:T(256)}, f32[256]{0:T(256)S(1)}, u32[]{:S(2)}) copy-start(f32[256]{0:T(256)S(1)} %broadcast_multiply_fusion.2) | copy-start | bytes 3076
  31.7 69.0 %copy-start.76 = (f32[256]{0:T(256)}, f32[256]{0:T(256)S(1)}, u32[]{:S(2)}) copy-start(f32[256]{0:T(256)S(1)} %fusion.53) | copy-start | bytes 3076
  31.7 69.0 %copy-start.72 = (f32[256]{0:T(256)}, f32[256]{0:T(256)S(1)}, u32[]{:S(2)}) copy-start(f32[256]{0:T(256)S(1)} %fusion.100) | copy-start | bytes 3076
  104.3 76.4 %all-to-all-start = ((bf16[3,1,256,1536]{2,0,1,3:T(4,128)(2,1)}), bf16[3,1,256,1536]{2,0,1,3:T(4,128)(2,1)}, u32[]{:S(2)}, u32[]{:S(2)}) async-start(bf16[3,1,256,1536]{2,0,1,3:T(4,128)(2,1)} %copy.187), calls=%async_computation | async-start | bytes 6291456 | tf_op jit(solution)/shard_map/all_to_all | solution.py:145
  187.2 8.9 copy-start.25
  189.2 14.4 copy-start.35
  195.1 7.3 copy-start.3
  195.1 7.3 copy-start.59
  196.6 5.9 copy-start.61
  216.4 23.5 %all-to-all-start.1 = ((bf16[4,2,49152]{2,1,0:T(2,128)(2,1)}), bf16[4,2,49152]{2,1,0:T(2,128)(2,1)S(1)}, u32[]{:S(2)}, u32[]{:S(2)}) async-start(bf16[4,2,49152]{2,1,0:T(2,128)(2,1)} %reshape.954), calls=%async_computation.1 | async-start | bytes 1572864 | tf_op jit(solution)/shard_map/all_to_all | solution.py:150
  220.0 317.6 %all-reduce.7.cloned.1.call-start = ((), (), s32[]{:S(2)}) async-start(), calls=%async_computation.18 | async-start | bytes 786432 | tf_op jit(solution)/shard_map/psum | solution.py:212
  245.5 5.2 copy-start.80
  245.8 4.8 copy-start.78
  245.8 6.3 copy-start.34
  254.0 237.8 %copy-start.58 = (f32[24,256]{1,0:T(8,128)}, f32[24,256]{1,0:T(8,128)S(1)}, u32[]{:S(2)}) copy-start(f32[24,256]{1,0:T(8,128)S(1)} %get-tuple-element.189) | copy-start | bytes 73732
  260.8 218.7 %copy-start.9 = (f32[1,256,1536]{2,1,0:T(8,128)}, f32[1,256,1536]{2,1,0:T(8,128)S(1)}, u32[]{:S(2)}) copy-start(f32[1,256,1536]{2,1,0:T(8,128)S(1)} %get-tuple-element.192) | copy-start | bytes 4718596
  480.0 7.1 copy-start.74
  482.3 7.1 copy-start.31
  500.4 396.8 %reduce-scatter.31.cloned.1.call-start = ((), (), s32[]{:S(2)}) async-start(), calls=%async_computation.26 | async-start | bytes 15925248
  595.6 9.2 slice-start.3
  596.7 8.1 slice-start.4
  607.4 13.0 copy-start.60
  607.5 13.0 copy-start.62
  607.5 13.0 copy-start.53
  607.5 13.0 copy-start.64
  616.7 22.0 %all-to-all-start.2 = ((bf16[4,2,49152]{2,1,0:T(2,128)(2,1)}), bf16[4,2,49152]{2,1,0:T(2,128)(2,1)S(1)}, u32[]{:S(2)}, u32[]{:S(2)}) async-start(bf16[4,2,49152]{2,1,0:T(2,128)(2,1)} %reshape.956), calls=%async_computation.2 | async-start | bytes 1572864 | tf_op jit(solution)/shard_map/all_to_all | solution.py:234
  620.5 326.3 %reduce-scatter.29.cloned.1.call-start = ((), (), s32[]{:S(2)}) async-start(), calls=%async_computation.25 | async-start | bytes 15925248
  641.0 13.3 copy-start.21
  645.1 9.1 copy-start.42
  654.2 14.7 slice-start
  654.2 14.7 slice-start.1
  661.2 6.7 copy-start.28
  661.2 7.8 slice-start.2
  696.9 6.1 copy-start.32
  696.9 6.1 copy-start.33
  845.6 158.8 %reduce-scatter.19.cloned.1.call-start = ((), (), s32[]{:S(2)}) async-start(), calls=%async_computation.20 | async-start | bytes 5308416 | tf_op jit(solution)/shard_map/reduce_scatter | solution.py:224
  851.5 210.8 %reduce-scatter.17.cloned.1.call-start = ((), (), s32[]{:S(2)}) async-start(), calls=%async_computation.19 | async-start | bytes 5308416 | tf_op jit(solution)/shard_map/reduce_scatter | solution.py:252
  857.6 334.7 %reduce-scatter.21.cloned.1.call-start = ((), (), s32[]{:S(2)}) async-start(), calls=%async_computation.21 | async-start | bytes 21233664 | tf_op jit(solution)/shard_map/reduce_scatter | solution.py:189
  870.8 451.5 %reduce-scatter.23.cloned.1.call-start = ((), (), s32[]{:S(2)}) async-start(), calls=%async_computation.22 | async-start | bytes 21233664 | tf_op jit(solution)/shard_map/reduce_scatter | solution.py:192
  882.3 476.8 %reduce-scatter.25.cloned.1.call-start = ((), (), s32[]{:S(2)}) async-start(), calls=%async_computation.23 | async-start | bytes 442368
  885.5 7.6 copy-start.77
  895.9 500.1 %reduce-scatter.27.cloned.1.call-start = ((), (), s32[]{:S(2)}) async-start(), calls=%async_computation.24 | async-start | bytes 442368
  897.0 814.8 %all-reduce.9.cloned.1.call-start = ((), (), s32[]{:S(2)}) async-start(), calls=%async_computation.27 | async-start | bytes 18087936 | tf_op jit(solution)/shard_map/psum | solution.py:263
  901.0 50.9 %copy-start.17 = (bf16[192,3,1536]{2,1,0:T(4,128)(2,1)}, bf16[192,3,1536]{2,1,0:T(4,128)(2,1)S(1)}, u32[]{:S(2)}) copy-start(bf16[192,3,1536]{2,1,0:T(4,128)(2,1)S(1)} %reshape.947) | copy-start | bytes 5308420
  1323.7 10.7 copy-start.43
  1334.4 7.6 copy-start.12
  1334.4 7.6 copy-start.16
  1342.0 67.9 %copy-start.18 = (bf16[192,3,1536]{2,1,0:T(4,128)(2,1)S(1)}, bf16[192,3,1536]{2,1,0:T(4,128)(2,1)}, u32[]{:S(2)}) copy-start(bf16[192,3,1536]{2,1,0:T(4,128)(2,1)} %copy-done.17) | copy-start | bytes 5308420
  1711.8 5.6 copy-start.48
  1721.3 5.8 copy-start.39
  (51 other events, 138.5 us)
Sparse Core Ops, SparseCore 0:
  9.9 81.4 all-gather.8
  93.3 78.6 all-gather.12
  173.8 38.7 all-gather.10
  214.4 38.7 all-gather.14
  255.0 98.5 all-gather.16
  355.3 98.5 all-gather.18
  500.6 36.9 all-reduce.6
  595.7 101.5 reduce-scatter.30
  845.8 100.9 reduce-scatter.28
  950.6 53.7 reduce-scatter.18
  1008.5 53.7 reduce-scatter.16
  1065.8 126.4 reduce-scatter.20
  1195.8 126.4 reduce-scatter.22
  1325.2 33.8 reduce-scatter.24
  1362.0 33.8 reduce-scatter.26
  1399.6 312.1 all-reduce.8
where the time goes:
time: 1750 us; the launch traced here: 1740 us
  waiting for transfers between devices  1110 us (63%)
  matrix products  220 us (13%)
  local copies, waits for them, and re-layouts  207 us (12%)
  blocking collectives  104 us (6%)
  other arithmetic  70.1 us (4%)
    psum x1, waiting for transfers between devices, body(): lax.psum(project_share.astype(jnp.bfloat16), 'seq').astype(jnp.float32)  297 us
    dot_general x38, matrix products, contract(): return jnp.einsum(form, left, right, preferred_element_type=jnp.float32)  218 us
    unnamed x214, local copies, waits for them, and re-layouts  146 us
    reduce_scatter x1, waiting for transfers between devices, body(): lax.psum_scatter(grad_down.astype(jnp.bfloat16), 'shard', scatter_dimensi...  130 us
    reduce_scatter x1, waiting for transfers between devices, body(): lax.psum_scatter(grad_up.astype(jnp.bfloat16), 'shard', scatter_dimension...  130 us
    unnamed x20, waiting for transfers between devices  95.5 us
    all_gather x1, waiting for transfers between devices, fetch_mlp(): lax.all_gather(up_weight, 'shard', axis=0, tiled=True)  92.5 us
    all_gather x1, waiting for transfers between devices, fetch_mlp(): lax.all_gather(down_weight, 'shard', axis=0, tiled=True)  76.7 us
  transfers between devices with their start and end apart: 19, of which 15 were waited for; matrix products, arithmetic and copies ran while one was open for 21% of the time, Pallas kernels for 0%

commit v1 on v0

--- a/solution.py
+++ b/solution.py
@@ -7,6 +7,28 @@
 QBLOCK = 512
 EPSILON = 1e-05
 MASKED_SCORE = -1e30
+
+
+def laid_out(blocks, dim):
+    shape = list(blocks.shape[1:])
+    shape[dim] *= blocks.shape[0]
+    return jnp.moveaxis(blocks, 0, dim).reshape(shape)
+
+
+def doubled(x, axis):
+    size = lax.axis_size(axis)
+    blocks = x[None]
+    for level in range(size.bit_length() - 1):
+        apart = 1 << level
+        other = lax.ppermute(blocks, axis, [(i, i ^ apart) for i in range(size)])
+        both = jnp.stack([blocks, other])
+        upper = lax.axis_index(axis) >> level & 1
+        blocks = jnp.where(upper == 0, both, both[::-1]).reshape(-1, *x.shape)
+    return blocks
+
+
+def gather_by_bits(x, axis, dim):
+    return laid_out(doubled(x, axis), dim)
 
 
 def layer_norm(hidden, gain, shift):
@@ -115,7 +137,7 @@
 def fetch_mlp(up_weight, down_weight):
     return (
         lax.all_gather(up_weight, "shard", axis=0, tiled=True),
-        lax.all_gather(down_weight, "shard", axis=0, tiled=True),
+        gather_by_bits(down_weight, "shard", 0),
     )
 
 

time: 1750 us -> 2080 us (1.19)
  blocking collectives: 104 us -> 428 us
  waiting for transfers between devices: 1110 us -> 1030 us
  other arithmetic: 70.1 us -> 140 us
    all_gather x1, blocking collectives: 10.4 us -> 335 us  [fetch_self(): lax.all_gather(norm_gain, 'shard', axis=1, tiled=True)]
    ppermute x0 -> x3, waiting for transfers between devices: none -> 180 us  [doubled(): other = lax.ppermute(blocks, axis, [(i, i ^ apart) for i in range(size)])]
    all_gather x1, waiting for transfers between devices: 92.5 us -> 0.02 us  [fetch_mlp(): lax.all_gather(up_weight, 'shard', axis=0, tiled=True)]
    all_gather x1 -> x0, waiting for transfers between devices: 76.7 us -> none  [fetch_mlp(): lax.all_gather(down_weight, 'shard', axis=0, tiled=True)]
    all_gather x1, waiting for transfers between devices: 59.6 us -> 0.02 us  [fetch_self(): lax.all_gather(self_project, 'shard', axis=1, tiled=True)]
    select_n x0 -> x2, other arithmetic: none -> 36.1 us  [doubled(): blocks = jnp.where(upper == 0, both, both[::-1]).reshape(-1, *x.shape)]
    another operation x2 -> x6, other arithmetic: 1.03 us -> 34.8 us  [the longest x4 33.7 us: doubled(): both = jnp.stack([blocks, other])]
    unnamed x20 -> x19, waiting for transfers between devices: 95.5 us -> 95.2 us
  transfers between devices with their start and end apart: 19 -> 21, of which waited for: 15 -> 13; matrix products, arithmetic and copies ran while one was open for 21% -> 20% of each run, Pallas kernels for 0% -> 0%
where the time goes in v1:
time: 2080 us; the launch traced here: 2070 us
  waiting for transfers between devices  1030 us (50%)
  blocking collectives  428 us (21%)
  matrix products  226 us (11%)
  local copies, waits for them, and re-layouts  207 us (10%)
  other arithmetic  140 us (7%)
    all_gather x1, blocking collectives, fetch_self(): lax.all_gather(norm_gain, 'shard', axis=1, tiled=True)  335 us
    psum x1, waiting for transfers between devices, body(): lax.psum(project_share.astype(jnp.bfloat16), 'seq').astype(jnp.float32)  297 us
    dot_general x38, matrix products, contract(): return jnp.einsum(form, left, right, preferred_element_type=jnp.float32)  225 us
    ppermute x3, waiting for transfers between devices, doubled(): other = lax.ppermute(blocks, axis, [(i, i ^ apart) for i in range(size)])  180 us
    unnamed x218, local copies, waits for them, and re-layouts  147 us
    reduce_scatter x1, waiting for transfers between devices, body(): lax.psum_scatter(grad_up.astype(jnp.bfloat16), 'shard', scatter_dimension...  130 us
    reduce_scatter x1, waiting for transfers between devices, body(): lax.psum_scatter(grad_down.astype(jnp.bfloat16), 'shard', scatter_dimensi...  130 us
    unnamed x19, waiting for transfers between devices  95.2 us
  transfers between devices with their start and end apart: 21, of which 13 were waited for; matrix products, arithmetic and copies ran while one was open for 20% of the time, Pallas kernels for 0%

profile of v1, /device:TPU:0, one launch (start us, length us, event | category | flops | bytes accessed | tf_op | source)
XLA Modules:
  0.0 2066.7 jit_solution(1067788886525780577)
XLA Ops:
  11.2 4.3 collective-permute-done
  17.5 5.6 fusion.24
  25.8 175.3 %collective-permute-done.1 = bf16[2,768,1536]{2,1,0:T(8,128)(2,1)} collective-permute-done((bf16[2,768,1536]{2,1,0:T(8,128)(2,1)}, bf16[2,768,1536]{2,1,0:T(8,128)(2,1)}, u32[]{:S(2)}, u32[]{:S(2)}) %collective-permute-start.1) | collective-permute-done | bytes 4718624 | tf_op jit(solution)/shard_map/ppermute | solution.py:23
  201.0 9.3 pad_maximum_fusion.2
  210.3 13.1 reverse_select_fusion.1
  225.4 335.2 %all-gather = bf16[8,192,3]{1,2,0:T(4,128)(2,1)S(1)} all-gather(bf16[1,192,3]{1,2,0:T(4,128)(2,1)S(1)} %bitcast.389), channel_id=1, replica_groups=mesh['seq'=4,'shard'=8] {'shard'}, dimensions={0}, use_global_device_ids=true | all-gather | bytes 10368 | tf_op jit(solution)/shard_map/all_gather | solution.py:125
  560.6 8.0 all-gather.1
  569.5 9.3 fusion.29
  582.4 5.1 all-to-all-start
  589.5 16.8 pad_maximum_fusion
  606.2 52.8 %all-to-all-done = bf16[3,1,256,1536]{2,0,1,3:T(4,128)(2,1)} async-done(((bf16[3,1,256,1536]{2,0,1,3:T(4,128)(2,1)}), bf16[3,1,256,1536]{2,0,1,3:T(4,128)(2,1)}, u32[]{:S(2)}, u32[]{:S(2)}) %all-to-all-start) | async-done | bytes 2359328 | tf_op jit(solution)/shard_map/all_to_all | solution.py:167
  659.0 4.1 copy.251
  688.0 5.5 reduce.59
  698.1 23.0 %reverse_select_fusion = bf16[2,4,768,1536]{3,2,1,0:T(8,128)(2,1)} fusion(bf16[2,4,768,1536]{3,2,1,0:T(8,128)(2,1)} %pad_maximum_fusion, pred[]{:T(512)S(6)} %eq.12), kind=kLoop, calls=%fused_computation.1 | loop fusion | flops 9437184 | bytes 37748736 | tf_op jit(solution)/shard_map/jit(_where)/select_n | solution.py:26
  721.0 5.4 fusion.43
  729.6 4.1 fusion.119
  734.1 4.7 fusion.34
  749.3 24.1 %multiply_convert_fusion.2 = (bf16[256,6144]{1,0:T(8,128)(2,1)}, f32[256,6144]{1,0:T(8,128)}, f32[256,6144]{1,0:T(8,128)}) fusion(bf16[1536,6144]{1,0:T(8,128)(2,1)} %all-gather.16.cloned.1.call-done, f32[1,256,1536]{2,1,0:T(8,128)S(1)} %get-tuple-element.194, f32[1536]{0:T(1024)S(1)} %get-tuple-element.161, f32[1536]{0:T(1024)S(1)} %get-tuple-element.208, ...), kind=kOutput, calls=%fused_computation.37 | convolution fusion | flops 4936040448 | bytes 36190208 | tf_op jit(solution)/shard_map/cfd,dk->cfk/dot_general | solution.py:45
  773.4 21.4 %add_convert_fusion = bf16[256,6144]{1,0:T(8,128)(2,1)S(1)} fusion(f32[256,6144]{1,0:T(8,128)} %get-tuple-element.177, bf16[6144,1536]{1,0:T(8,128)(2,1)} %bitcast.348, f32[256,6144]{1,0:T(8,128)} %get-tuple-element.195, bf16[1,256,1536]{2,1,0:T(8,128)(2,1)S(1)} %copy-done.19), kind=kOutput, calls=%fused_computation.36 | convolution fusion | flops 4853858304 | bytes 35389440 | tf_op jit(solution)/shard_map/cfd,kd->cfk/dot_general | solution.py:45
  794.8 11.0 fusion.59
  808.7 4.8 convolution_convert_fusion.8
  832.9 6.8 copy.218
  839.7 24.7 %all-reduce.7.cloned.1.call-done = bf16[2,64,1536]{2,1,0:T(8,128)(2,1)} async-done(((bf16[2,64,1536]{2,1,0:T(8,128)(2,1)}), bf16[2,64,1536]{2,1,0:T(8,128)(2,1)}) %all-reduce.7.cloned.1.call-update) | async-done | bytes 393232 | tf_op jit(solution)/shard_map/psum | solution.py:234
  868.4 6.1 pad_maximum_fusion.1
  874.5 30.8 %copy.233 = bf16[3,1536,1536]{2,0,1:T(4,128)(2,1)} copy(bf16[3,1536,1536]{1,2,0:T(8,128)(2,1)} %pad_maximum_fusion.1) | data formatting | bytes 28311552
  905.3 17.0 copy.241
  923.5 4.3 fusion.60
  934.3 8.2 reduce.60
  947.3 18.2 all-to-all-done.2
  967.8 4.2 fusion.66
  972.0 6.2 fusion.57
  981.1 6.9 multiply_reduce_fusion.1
  988.0 6.7 multiply_convert_fusion.1
  996.2 6.8 multiply_reduce_fusion
  1003.0 6.2 multiply_convert_fusion
  1012.1 5.2 copy.211
  1019.0 4.9 fusion.76
  1024.9 5.1 copy.210
  1030.0 6.8 pad_maximum_fusion.4
  1036.8 72.8 %all_to_all.60 = bf16[3,1,1024,384]{3,0,1,2:T(4,128)(2,1)S(1)} all-to-all(bf16[3,1,1024,384]{3,0,1,2:T(4,128)(2,1)S(1)} %pad_maximum_fusion.4), channel_id=1, replica_groups=mesh['seq'=4,'shard'=8] {'seq'}, dimensions={2} | all-to-all | bytes 4718592 | tf_op jit(solution)/shard_map/all_to_all | solution.py:263
  1113.2 4.1 reshape.938
  1117.3 7.5 convert_bitcast_fusion
  1124.8 30.8 %copy.231 = bf16[3,1536,1536]{2,0,1:T(4,128)(2,1)} copy(bf16[3,1536,1536]{1,2,0:T(8,128)(2,1)} %convert_bitcast_fusion) | data formatting | bytes 28311552
  1155.6 17.1 copy.240
  1172.9 5.1 convolution_convert_fusion.3
  1178.1 6.1 convolution_convert_fusion.5
  1185.0 12.9 convolution_convert_fusion.1
  1197.9 11.4 convolution_convert_fusion
  1212.5 7.4 fusion.56
  1233.6 40.3 %reduce-scatter.29.cloned.1.call-done = bf16[192,4608]{1,0:T(8,128)(2,1)} async-done(((bf16[1536,4608]{1,0:T(8,128)(2,1)}), bf16[192,4608]{1,0:T(8,128)(2,1)}) %reduce-scatter.29.cloned.1.call-update) | async-done | bytes 1769488
  1273.9 5.2 reshape.955
  1279.0 5.5 copy.232
  1284.6 47.1 %reduce-scatter.19.cloned.1.call-done = bf16[192,1536]{1,0:T(8,128)(2,1)} async-done(((bf16[1536,1536]{1,0:T(8,128)(2,1)}), bf16[192,1536]{1,0:T(8,128)(2,1)}) %reduce-scatter.19.cloned.1.call-update) | async-done | bytes 589840 | tf_op jit(solution)/shard_map/reduce_scatter | solution.py:246
  1331.7 57.7 %reduce-scatter.17.cloned.1.call-done = bf16[192,1536]{1,0:T(8,128)(2,1)} async-done(((bf16[1536,1536]{1,0:T(8,128)(2,1)}), bf16[192,1536]{1,0:T(8,128)(2,1)}) %reduce-scatter.17.cloned.1.call-update) | async-done | bytes 589840 | tf_op jit(solution)/shard_map/reduce_scatter | solution.py:274
  1389.4 130.1 %reduce-scatter.21.cloned.1.call-done = bf16[192,6144]{1,0:T(8,128)(2,1)} async-done(((bf16[1536,6144]{1,0:T(8,128)(2,1)}), bf16[192,6144]{1,0:T(8,128)(2,1)}) %reduce-scatter.21.cloned.1.call-update) | async-done | bytes 2359312 | tf_op jit(solution)/shard_map/reduce_scatter | solution.py:211
  1519.5 129.9 %reduce-scatter.23.cloned.1.call-done = bf16[768,1536]{1,0:T(8,128)(2,1)} async-done(((bf16[6144,1536]{1,0:T(8,128)(2,1)}), bf16[768,1536]{1,0:T(8,128)(2,1)}) %reduce-scatter.23.cloned.1.call-update) | async-done | bytes 2359312 | tf_op jit(solution)/shard_map/reduce_scatter | solution.py:214
  1650.8 10.7 fusion.33
  1661.5 7.6 fusion.46
  1670.8 15.6 reduce-scatter.25.cloned.1.call-done
  1687.3 36.0 %reduce-scatter.27.cloned.1.call-done = bf16[192,3]{1,0:T(8,128)(2,1)} async-done(((bf16[1536,3]{1,0:T(8,128)(2,1)}), bf16[192,3]{1,0:T(8,128)(2,1)}) %reduce-scatter.27.cloned.1.call-update) | async-done | bytes 1168
  1724.2 11.9 all-reduce.2
  1742.1 297.0 %all-reduce.9.cloned.1.call-done = (bf16[3,192,1536]{1,2,0:T(8,128)(2,1)}, bf16[192,1536]{1,0:T(8,128)(2,1)}, bf16[1,192,1536]{1,2,0:T(8,128)(2,1)}, bf16[192,15...) async-done(((bf16[3,192,1536]{1,2,0:T(8,128)(2,1)}, bf16[192,1536]{1,0:T(8,128)(2,1)}, bf16[1,192,1536]{1,2,0:T(8,128)(2,1)}, ...) | async-done | bytes 8257552 | tf_op jit(solution)/shard_map/psum | solution.py:285
  2039.1 4.5 copy.219
  2048.6 5.7 copy.220
  (353 shorter events, 153.3 us)
Async XLA Ops:
  7.2 713.9 %copy-start = (bf16[1,64,1536]{2,1,0:T(8,128)(2,1)S(1)}, bf16[1,64,1536]{2,1,0:T(8,128)(2,1)}, u32[]{:S(2)}) copy-start(bf16[1,64,1536]{2,1,0:T(8,128)(2,1)} %param.24) | copy-start | bytes 589828
  7.2 562.2 %all-gather.8.cloned.1.call-start = ((), (), s32[]{:S(2)}) async-start(), calls=%async_computation.12 | async-start | bytes 15925248 | tf_op jit(solution)/shard_map/all_gather | solution.py:123
  7.9 713.1 %all-gather.12.cloned.1.call-start = ((), (), s32[]{:S(2)}) async-start(), calls=%async_computation.14 | async-start | bytes 15925248 | tf_op jit(solution)/shard_map/all_gather | solution.py:132
  8.7 720.9 %all-gather.10.cloned.1.call-start = ((), (), s32[]{:S(2)}) async-start(), calls=%async_computation.13 | async-start | bytes 5308416 | tf_op jit(solution)/shard_map/all_gather | solution.py:124
  9.4 735.5 %all-gather.14.cloned.1.call-start = ((), (), s32[]{:S(2)}) async-start(), calls=%async_computation.15 | async-start | bytes 5308416 | tf_op jit(solution)/shard_map/all_gather | solution.py:133
  10.0 739.3 %all-gather.16.cloned.1.call-start = ((), (), s32[]{:S(2)}) async-start(), calls=%async_computation.16 | async-start | bytes 21233664 | tf_op jit(solution)/shard_map/all_gather | solution.py:139
  10.6 4.9 collective-permute-start
  23.1 177.9 %collective-permute-start.1 = (bf16[2,768,1536]{2,1,0:T(8,128)(2,1)}, bf16[2,768,1536]{2,1,0:T(8,128)(2,1)}, u32[]{:S(2)}, u32[]{:S(2)}) collective-permute-start(bf16[2,768,1536]{2,1,0:T(8,128)(2,1)} %get-tuple-element.179), channel_id=1, source_target_pairs={{0,2},{1,3},{2,0},{3,1},{4,6},{5,7},{6,4},{7,5},{8,10},{9,11},{10,... | collective-permute-start | bytes 14155784 | tf_op jit(solution)/shard_map/ppermute | solution.py:23
  210.3 15.0 copy-start.91
  210.3 350.3 %copy-start.92 = (bf16[3,192]{1,0:T(4,128)(2,1)S(1)}, bf16[3,192]{1,0:T(4,128)(2,1)}, u32[]{:S(2)}) copy-start(bf16[3,192]{1,0:T(4,128)(2,1)} %param.26) | copy-start | bytes 3460
  210.3 358.4 %copy-start.5 = (bf16[1,256,1536]{2,1,0:T(8,128)(2,1)S(1)}, bf16[1,256,1536]{2,1,0:T(8,128)(2,1)}, u32[]{:S(2)}) copy-start(bf16[1,256,1536]{2,1,0:T(8,128)(2,1)} %param.23) | copy-start | bytes 2359300
  223.4 366.0 %collective-permute-start.2 = (bf16[4,768,1536]{2,1,0:T(8,128)(2,1)}, bf16[4,768,1536]{2,1,0:T(8,128)(2,1)}, u32[]{:S(2)}, u32[]{:S(2)}) collective-permute-start(bf16[4,768,1536]{2,1,0:T(8,128)(2,1)} %bitcast.346), channel_id=1, source_target_pairs={{0,4},{1,5},{2,6},{3,7},{4,0},{5,1},{6,2},{7,3},{8,12},{9,13},{10,... | collective-permute-start | bytes 28311560 | tf_op jit(solution)/shard_map/ppermute | solution.py:23
  568.8 10.0 copy-start.56
  568.8 10.0 copy-start.67
  568.8 165.3 %copy-start.69 = (f32[1536]{0:T(1024)}, f32[1536]{0:T(1024)S(1)}, u32[]{:S(2)}) copy-start(f32[1536]{0:T(1024)S(1)} %get-tuple-element.207) | copy-start | bytes 18436
  568.8 165.3 %copy-start.85 = (f32[1536]{0:T(1024)}, f32[1536]{0:T(1024)S(1)}, u32[]{:S(2)}) copy-start(f32[1536]{0:T(1024)S(1)} %get-tuple-element.162) | copy-start | bytes 18436
  568.8 180.5 %copy-start.58 = (f32[1536]{0:T(1024)}, f32[1536]{0:T(1024)S(1)}, u32[]{:S(2)}) copy-start(f32[1536]{0:T(1024)S(1)} %get-tuple-element.161) | copy-start | bytes 18436
  569.0 9.8 copy-start.72
  569.4 9.4 copy-start.78
  569.4 9.4 copy-start.74
  582.4 76.6 %all-to-all-start = ((bf16[3,1,256,1536]{2,0,1,3:T(4,128)(2,1)}), bf16[3,1,256,1536]{2,0,1,3:T(4,128)(2,1)}, u32[]{:S(2)}, u32[]{:S(2)}) async-start(bf16[3,1,256,1536]{2,0,1,3:T(4,128)(2,1)} %copy.193), calls=%async_computation | async-start | bytes 6291456 | tf_op jit(solution)/shard_map/all_to_all | solution.py:167
  665.4 8.9 copy-start.25
  667.4 14.1 copy-start.35
  673.3 6.9 copy-start.3
  673.3 6.9 copy-start.61
  694.5 33.9 %all-to-all-start.1 = ((bf16[4,2,49152]{2,1,0:T(2,128)(2,1)}), bf16[4,2,49152]{2,1,0:T(2,128)(2,1)S(1)}, u32[]{:S(2)}, u32[]{:S(2)}) async-start(bf16[4,2,49152]{2,1,0:T(2,128)(2,1)} %reshape.964), calls=%async_computation.1 | async-start | bytes 1572864 | tf_op jit(solution)/shard_map/all_to_all | solution.py:172
  698.0 166.4 %all-reduce.7.cloned.1.call-start = ((), (), s32[]{:S(2)}) async-start(), calls=%async_computation.17 | async-start | bytes 786432 | tf_op jit(solution)/shard_map/psum | solution.py:234
  734.1 6.2 copy-start.34
  742.2 76.0 %copy-start.60 = (f32[24,256]{1,0:T(8,128)}, f32[24,256]{1,0:T(8,128)S(1)}, u32[]{:S(2)}) copy-start(f32[24,256]{1,0:T(8,128)S(1)} %get-tuple-element.191) | copy-start | bytes 73732
  749.0 56.9 %copy-start.9 = (f32[1,256,1536]{2,1,0:T(8,128)}, f32[1,256,1536]{2,1,0:T(8,128)S(1)}, u32[]{:S(2)}) copy-start(f32[1,256,1536]{2,1,0:T(8,128)S(1)} %get-tuple-element.194) | copy-start | bytes 4718596
  749.3 24.1 %copy-start.19 = (bf16[1,256,1536]{2,1,0:T(8,128)(2,1)S(1)}, bf16[1,256,1536]{2,1,0:T(8,128)(2,1)}, u32[]{:S(2)}) copy-start(bf16[1,256,1536]{2,1,0:T(8,128)(2,1)} %param.33) | copy-start | bytes 2359300
  794.8 11.0 copy-start.38
  806.4 7.1 copy-start.76
  808.7 7.1 copy-start.31
  826.9 397.4 %reduce-scatter.31.cloned.1.call-start = ((), (), s32[]{:S(2)}) async-start(), calls=%async_computation.25 | async-start | bytes 15925248
  922.4 9.2 slice-start.3
  923.5 8.1 slice-start.4
  934.3 13.0 copy-start.62
  934.3 13.0 copy-start.64
  934.3 13.0 copy-start.55
  934.3 13.0 copy-start.66
  943.5 22.0 %all-to-all-start.2 = ((bf16[4,2,49152]{2,1,0:T(2,128)(2,1)}), bf16[4,2,49152]{2,1,0:T(2,128)(2,1)S(1)}, u32[]{:S(2)}, u32[]{:S(2)}) async-start(bf16[4,2,49152]{2,1,0:T(2,128)(2,1)} %reshape.966), calls=%async_computation.2 | async-start | bytes 1572864 | tf_op jit(solution)/shard_map/all_to_all | solution.py:256
  947.3 326.6 %reduce-scatter.29.cloned.1.call-start = ((), (), s32[]{:S(2)}) async-start(), calls=%async_computation.24 | async-start | bytes 15925248
  967.8 13.3 copy-start.21
  972.0 9.1 copy-start.44
  981.1 14.7 slice-start
  981.1 14.8 slice-start.1
  988.0 6.7 copy-start.28
  988.0 7.8 slice-start.2
  1023.9 6.1 copy-start.32
  1023.9 6.1 copy-start.33
  1172.7 159.0 %reduce-scatter.19.cloned.1.call-start = ((), (), s32[]{:S(2)}) async-start(), calls=%async_computation.19 | async-start | bytes 5308416 | tf_op jit(solution)/shard_map/reduce_scatter | solution.py:246
  1178.0 211.3 %reduce-scatter.17.cloned.1.call-start = ((), (), s32[]{:S(2)}) async-start(), calls=%async_computation.18 | async-start | bytes 5308416 | tf_op jit(solution)/shard_map/reduce_scatter | solution.py:274
  1184.3 335.2 %reduce-scatter.21.cloned.1.call-start = ((), (), s32[]{:S(2)}) async-start(), calls=%async_computation.20 | async-start | bytes 21233664 | tf_op jit(solution)/shard_map/reduce_scatter | solution.py:211
  1197.9 451.6 %reduce-scatter.23.cloned.1.call-start = ((), (), s32[]{:S(2)}) async-start(), calls=%async_computation.21 | async-start | bytes 21233664 | tf_op jit(solution)/shard_map/reduce_scatter | solution.py:214
  1209.3 477.1 %reduce-scatter.25.cloned.1.call-start = ((), (), s32[]{:S(2)}) async-start(), calls=%async_computation.22 | async-start | bytes 442368
  1212.5 7.6 copy-start.79
  1222.9 500.4 %reduce-scatter.27.cloned.1.call-start = ((), (), s32[]{:S(2)}) async-start(), calls=%async_computation.23 | async-start | bytes 442368
  1224.0 815.1 %all-reduce.9.cloned.1.call-start = ((), (), s32[]{:S(2)}) async-start(), calls=%async_computation.26 | async-start | bytes 18087936 | tf_op jit(solution)/shard_map/psum | solution.py:285
  1228.1 51.0 %copy-start.17 = (bf16[192,3,1536]{2,1,0:T(4,128)(2,1)}, bf16[192,3,1536]{2,1,0:T(4,128)(2,1)S(1)}, u32[]{:S(2)}) copy-start(bf16[192,3,1536]{2,1,0:T(4,128)(2,1)S(1)} %reshape.957) | copy-start | bytes 5308420
  1650.8 10.7 copy-start.45
  1661.5 7.6 copy-start.12
  1661.5 7.6 copy-start.16
  1669.2 68.1 %copy-start.18 = (bf16[192,3,1536]{2,1,0:T(4,128)(2,1)S(1)}, bf16[192,3,1536]{2,1,0:T(4,128)(2,1)}, u32[]{:S(2)}) copy-start(bf16[192,3,1536]{2,1,0:T(4,128)(2,1)} %copy-done.17) | copy-start | bytes 5308420
  (55 other events, 164.1 us)
Sparse Core Ops, SparseCore 0:
  9.9 133.7 all-gather.7
  145.6 111.1 all-gather.11
  258.7 57.8 all-gather.9
  318.4 57.9 all-gather.13
  378.1 174.6 all-gather.15
  827.0 37.3 all-reduce.6
  922.6 101.5 reduce-scatter.30
  1172.8 101.0 reduce-scatter.28
  1277.9 53.7 reduce-scatter.18
  1335.6 53.7 reduce-scatter.16
  1393.0 126.4 reduce-scatter.20
  1523.0 126.4 reduce-scatter.22
  1652.5 33.9 reduce-scatter.24
  1689.4 33.8 reduce-scatter.26
  1727.0 312.0 all-reduce.8
